TPU v7x, 32 devices: a whole 2x2x4 slice. The times are simulated.
32 devices in a mesh: fsdp: 2 (over y), rows: 8 (over z, core), cols: 2 (over x).
Axes of the slice: x: 2, y: 2, z: 4, core: 2. Of those that a mesh axis runs over, the one named last changes fastest.
Arguments:
- image: bfloat16 [2, 128, 256, 128], P('fsdp', 'rows', 'cols'), may hold values from -6 to 6
- dw_kernel: float32 [7, 7, 128], replicated, may hold values from -0.875 to 0.875
- dw_bias: float32 [128], replicated, may hold values from -3 to 3
- layer_norm_gain: float32 [128], replicated, may hold values from 0.1 to 1.9
- layer_norm_bias: float32 [128], replicated, may hold values from -3 to 3
- w_in: bfloat16 [128, 512], P('fsdp'), may hold values from -0.5 to 0.5
- b_in: float32 [512], replicated, may hold values from -3 to 3
- w_out: bfloat16 [512, 128], P('fsdp'), may hold values from -0.25 to 0.25
- b_out: float32 [128], replicated, may hold values from -3 to 3
- cotangent: bfloat16 [2, 128, 256, 128], P('fsdp', 'rows', 'cols'), may hold values from -60 to 60
Outputs:
- mixed: bfloat16 [2, 128, 256, 128], P('fsdp', 'rows', 'cols')
- d_image: bfloat16 [2, 128, 256, 128], P('fsdp', 'rows', 'cols')
- g_w_in: float32 [128, 512], P('fsdp')
- g_w_out: float32 [512, 128], P('fsdp')
- g_b_in: float32 [512], replicated
- g_kernel: float32 [7, 7, 128], replicated
- g_gain: float32 [128], replicated
All inputs are finite; a program needn't handle non-finite values.
Results may differ from a plain program's by a relative error of at most 0.0057.
Values may be sent and summed in bfloat16 or wider, within the bound.
No kernel may reach another device: no remote copies, remote signals or barrier semaphores. Data moves between devices by JAX's collectives and lax.ppermute only.
A program may use at most 64 MiB of HBM per device.

v0:
```python
import math

import jax
import jax.numpy as jnp
from jax import lax
from jax.sharding import PartitionSpec as P

norm_eps = 1e-06
gelu_coef = math.sqrt(2.0 / math.pi)
cubic_coef = 0.044715


def padded_2(shard, sides, width):
    for axis, dim in sides:
        devices, length = (lax.axis_size(axis), shard.shape[dim])
        up = [(i, (i + 1) % devices) for i in range(devices - 1)]
        down = [(j, i) for i, j in up]
        last = lax.slice_in_dim(shard, length - width, length, axis=dim)
        leading = lax.slice_in_dim(shard, 0, width, axis=dim)
        before = lax.ppermute(last, axis, up)
        after = lax.ppermute(leading, axis, down)
        shard = jnp.concatenate([before, shard, after], axis=dim)
    return shard


def depthwise_taps(padded, kernel, height, width):
    total = jnp.zeros((height, width, padded.shape[2]), jnp.float32)
    for row_tap in range(7):
        for col_tap in range(7):
            total = (
                total
                + padded[row_tap : row_tap + height, col_tap : col_tap + width]
                * kernel[row_tap, col_tap]
            )
    return total


def transposed_taps(padded, kernel, height, width):
    total = jnp.zeros((height, width, padded.shape[2]), jnp.float32)
    for row_tap in range(7):
        for col_tap in range(7):
            total = (
                total
                + padded[6 - row_tap : 6 - row_tap + height, 6 - col_tap : 6 - col_tap + width]
                * kernel[row_tap, col_tap]
            )
    return total


def gelu_parts(pre):
    inner = gelu_coef * (pre + cubic_coef * pre * pre * pre)
    tanh_val = jnp.tanh(inner)
    value = 0.5 * pre * (1.0 + tanh_val)
    slope = 0.5 * (1.0 + tanh_val) + 0.5 * pre * (1.0 - tanh_val * tanh_val) * gelu_coef * (
        1.0 + 3.0 * cubic_coef * pre * pre
    )
    return (value, slope)


def extend_image(field):
    return padded_2(field, (("rows", 0), ("cols", 1)), 3)


def extend_grad(field):
    return padded_2(field, (("rows", 0), ("cols", 1)), 3)


def on_device(
    image, dw_kernel, dw_bias, layer_norm_gain, layer_norm_bias, w_in, b_in, w_out, b_out, cotangent
):
    contract_rows = (((0,), (0,)), ((), ()))
    contract_cols = (((1,), (1,)), ((), ()))
    field = image[0]
    upstream = cotangent[0]
    height, width, channel_count = field.shape
    padded_f = extend_image(field).astype(jnp.float32)
    conv = depthwise_taps(padded_f, dw_kernel, height, width) + dw_bias
    center = jnp.mean(conv, axis=-1, keepdims=True)
    variance_spread = conv - center
    inverse_deviation = lax.rsqrt(
        jnp.mean(variance_spread * variance_spread, axis=-1, keepdims=True) + norm_eps
    )
    standardized_input = variance_spread * inverse_deviation
    normalized_input = (
        (standardized_input * layer_norm_gain + layer_norm_bias)
        .astype(jnp.bfloat16)
        .reshape(-1, channel_count)
    )
    full_in, full_out = (
        lax.all_gather(w_in, "fsdp", axis=0, tiled=True),
        lax.all_gather(w_out, "fsdp", axis=0, tiled=True),
    )
    pre = jnp.dot(normalized_input, full_in, preferred_element_type=jnp.float32) + b_in
    value, slope = gelu_parts(pre)
    hidden = value.astype(jnp.bfloat16)
    mixed = (
        field.reshape(-1, channel_count).astype(jnp.float32)
        + jnp.dot(hidden, full_out, preferred_element_type=jnp.float32)
        + b_out
    )
    mixed = mixed.astype(jnp.bfloat16).reshape(height, width, channel_count)
    flat_up = upstream.reshape(-1, channel_count)
    d_hidden = lax.dot_general(flat_up, full_out, contract_cols, preferred_element_type=jnp.float32)
    d_pre = (d_hidden * slope).astype(jnp.bfloat16)
    normalized_gradient = lax.dot_general(
        d_pre, full_in, contract_cols, preferred_element_type=jnp.float32
    ).reshape(height, width, channel_count)
    gain_product = jnp.sum(normalized_gradient * standardized_input, axis=(0, 1))
    centered_scaled_gradient = normalized_gradient * layer_norm_gain
    convolution_gradient = (
        inverse_deviation
        * (
            centered_scaled_gradient
            - jnp.mean(centered_scaled_gradient, axis=-1, keepdims=True)
            - standardized_input
            * jnp.mean(centered_scaled_gradient * standardized_input, axis=-1, keepdims=True)
        )
    ).astype(jnp.bfloat16)
    bias_term = jnp.sum(d_pre.astype(jnp.float32), axis=0)
    grad_padded = extend_grad(convolution_gradient).astype(jnp.float32)
    d_image = (
        upstream.astype(jnp.float32) + transposed_taps(grad_padded, dw_kernel, height, width)
    ).astype(jnp.bfloat16)
    conv_grad = convolution_gradient.astype(jnp.float32)
    kernel_rows = []
    for row_tap in range(7):
        for col_tap in range(7):
            kernel_rows.append(
                jnp.sum(
                    padded_f[row_tap : row_tap + height, col_tap : col_tap + width] * conv_grad,
                    axis=(0, 1),
                )
            )
    kernel_term = jnp.stack(kernel_rows).reshape(7, 7, channel_count)
    in_rows = w_in.shape[0]
    out_rows = w_out.shape[0]
    term_in = lax.dot_general(
        normalized_input, d_pre, contract_rows, preferred_element_type=jnp.float32
    )
    term_out = lax.dot_general(hidden, flat_up, contract_rows, preferred_element_type=jnp.float32)
    total_in, total_out, g_b_in, g_kernel, g_gain = lax.psum(
        (term_in, term_out, bias_term, kernel_term, gain_product), ("fsdp", "rows", "cols")
    )
    owner = lax.axis_index("fsdp")
    g_w_in = lax.dynamic_slice_in_dim(total_in, owner * in_rows, in_rows, 0)
    g_w_out = lax.dynamic_slice_in_dim(total_out, owner * out_rows, out_rows, 0)
    return (mixed[None], d_image[None], g_w_in, g_w_out, g_b_in, g_kernel, g_gain)


def solution(mesh):
    return jax.shard_map(
        on_device,
        mesh=mesh,
        in_specs=(
            P("fsdp", "rows", "cols", None),
            P(),
            P(),
            P(),
            P(),
            P("fsdp", None),
            P(),
            P("fsdp", None),
            P(),
            P("fsdp", "rows", "cols", None),
        ),
        out_specs=(
            P("fsdp", "rows", "cols", None),
            P("fsdp", "rows", "cols", None),
            P("fsdp", None),
            P("fsdp", None),
            P(),
            P(),
            P(),
        ),
        check_vma=False,
    )
```

profile of v0, /device:TPU:1, one launch (start us, length us, event | category | flops | bytes accessed | tf_op | source)
XLA Modules:
  0.0 207.5 jit_solution(18088232705827283579)
XLA Ops:
  7.2 0.0 all-reduce.4.cloned.1.call-start
  7.2 1.0 slice_bitcast_fusion.1
  8.2 4.6 %collective-permute-start = (bf16[3,128,128]{2,1,0:T(8,128)(2,1)S(1)}, bf16[3,128,128]{2,1,0:T(8,128)(2,1)S(1)}, u32[]{:S(2)}, u32[]{:S(2)}) collective-permute-start(bf16[3,128,128]{2,1,0:T(8,128)(2,1)S(1)} %get-tuple-element.72), channel_id=1, source_target_pairs={{0,2},{2,4},{4,6},{6,8},{8,10},{10,12},{12,14},{1,3},{3,5},{5,7},{... | collective-permute-start | bytes 294920 | tf_op jit(solution)/shard_map/ppermute | solution.py:20
  12.8 1.9 collective-permute-start.1
  14.7 1.0 slice_bitcast_fusion.49
  15.7 1.0 slice_bitcast_fusion.50
  16.7 0.9 slice_bitcast_fusion.48
  17.6 4.0 %all_gather.6 = bf16[128,512]{1,0:T(8,128)(2,1)S(1)} all-gather(bf16[64,512]{1,0:T(8,128)(2,1)} %param.15), channel_id=1, replica_groups=mesh['fsdp'=2,'rows'=8,'cols'=2] {'fsdp'}, dimensions={0}, use_global_device_ids=true | all-gather | bytes 196608 | tf_op jit(solution)/shard_map/all_gather | solution.py:90
  21.6 0.0 collective-permute-done
  21.6 0.0 collective-permute-done.1
  21.6 0.8 pad_maximum_fusion.5
  22.4 3.1 %collective-permute-start.2 = (bf16[22,3,128]{2,1,0:T(4,128)(2,1)S(1)}, bf16[22,3,128]{2,1,0:T(4,128)(2,1)S(1)}, u32[]{:S(2)}, u32[]{:S(2)}) collective-permute-start(bf16[22,3,128]{2,1,0:T(4,128)(2,1)S(1)} %get-tuple-element.68), channel_id=1, source_target_pairs={{0,1},{2,3},{4,5},{6,7},{8,9},{10,11},{12,13},{14,15},{16,17},{18,... | collective-permute-start | bytes 50696 | tf_op jit(solution)/shard_map/ppermute | solution.py:20
  25.5 1.3 collective-permute-start.3
  26.8 4.8 %all_gather.7 = bf16[512,128]{1,0:T(8,128)(2,1)S(1)} all-gather(bf16[256,128]{1,0:T(8,128)(2,1)} %param.17), channel_id=1, replica_groups=mesh['fsdp'=2,'rows'=8,'cols'=2] {'fsdp'}, dimensions={0}, use_global_device_ids=true | all-gather | bytes 196608 | tf_op jit(solution)/shard_map/all_gather | solution.py:91
  31.6 0.0 collective-permute-done.2
  31.6 0.0 collective-permute-done.3
  31.7 1.3 maximum_convert_fusion
  32.9 0.0 copy-start.4
  32.9 0.0 copy-start.5
  32.9 0.0 copy-start.7
  32.9 8.2 %fusion.109 = (f32[16,128]{1,0:T(8,128)S(1)}, f32[16,128,128]{2,1,0:T(8,128)S(1)}) fusion(f32[128]{0:T(128)} %param.12, f32[128]{0:T(128)S(1)} %get-tuple-element.121, f32[22,134,128]{2,1,0:T(8,128)S(1)} %maximum_convert_fusion, f32[128]{0:T(128)S(1)} %get-tuple-element.122, f32[128]{0:T(128)S(1)} %get-tuple-element.75, f32[128]{0:T(128)S(1)} %get-tuple-element.76, ...), kind=kLoop, calls=%fused_computation.285 | loop fusion | flops 25950208 | bytes 52462592 | tf_op jit(solution)/shard_map/reduce_sum | solution.py:78
  41.2 0.6 multiply_reduce_fusion.3
  41.8 0.0 copy-done.4
  41.8 0.0 copy-done.5
  41.8 0.6 add_convert_fusion
  42.5 0.0 copy-done.7
  42.5 0.0 copy-start.2
  42.5 1.8 multiply_convert_fusion
  44.3 0.0 copy-start
  44.3 0.0 copy-done.2
  44.3 3.1 %convert_reduce_fusion = (f32[512]{0:T(512)S(1)}, bf16[2048,512]{1,0:T(8,128)(2,1)S(1)}) fusion(f32[2048,512]{1,0:T(8,128)S(1)} %get-tuple-element.124, f32[512]{0:T(512)S(1)} %copy-done.7, bf16[2048,128]{1,0:T(8,128)(2,1)S(1)} %bitcast.186, bf16[512,128]{1,0:T(8,128)(2,1)S(1)} %all_gather.7), kind=kOutput, calls=%fused_computation.58 | convolution fusion | flops 291503616 | bytes 6950912 | tf_op jit(solution)/shard_map/dot_general | solution.py:103
  47.5 0.8 multiply_reduce_fusion.2
  48.3 1.0 multiply_reduce_fusion
  49.3 3.0 %fusion.56 = (f32[128]{0:T(128)S(1)}, f32[128]{0:T(128)S(1)}, f32[128]{0:T(128)S(1)}, f32[128]{0:T(128)S(1)}, f32[128]{0:T(128)S(1)}, /*index=5*/f32[128]{0:T(12...) fusion(f32[22,134,128]{2,1,0:T(8,128)S(1)} %maximum_convert_fus, ...), kind=kLoop, calls=%fused_computation.110 | loop fusion | flops 11794176 | bytes 21538304 | tf_op jit(solution)/shard_map/reduce_sum | solution.py:129
  52.3 2.4 %fusion.57 = (f32[128]{0:T(128)S(1)}, f32[128]{0:T(128)S(1)}, f32[128]{0:T(128)S(1)}, f32[128]{0:T(128)S(1)}, f32[128]{0:T(128)S(1)}, /*index=5*/f32[128]{0:T(12...) fusion(bf16[16,128,128]{2,1,0:T(8,128)(2,1)S(1)} %get-tuple-ele, ...), kind=kLoop, calls=%fused_computation.111 | loop fusion | flops 9697024 | bytes 19407872 | tf_op jit(solution)/shard_map/reduce_sum | solution.py:129
  54.8 1.7 fusion.55
  56.4 0.0 copy-start.1
  56.5 0.0 copy-start.6
  56.5 1.2 fusion.111
  57.7 5.4 %collective-permute-start.4 = (bf16[3,128,128]{2,1,0:T(8,128)(2,1)S(1)}, bf16[3,128,128]{2,1,0:T(8,128)(2,1)S(1)}, u32[]{:S(2)}, u32[]{:S(2)}) collective-permute-start(bf16[3,128,128]{2,1,0:T(8,128)(2,1)S(1)} %get-tuple-element.70), channel_id=1, source_target_pairs={{0,2},{2,4},{4,6},{6,8},{8,10},{10,12},{12,14},{1,3},{3,5},{5,7},{... | collective-permute-start | bytes 294920 | tf_op jit(solution)/shard_map/ppermute | solution.py:20
  63.0 1.9 collective-permute-start.5
  65.0 0.0 copy-done
  65.0 1.5 fusion.112
  66.4 0.0 copy-start.3
  66.5 0.0 all-reduce.4.cloned.1.call-update
  66.5 0.0 collective-permute-done.4
  66.5 2.5 %collective-permute-done.5 = bf16[3,128,128]{2,1,0:T(8,128)(2,1)S(1)} collective-permute-done((bf16[3,128,128]{2,1,0:T(8,128)(2,1)S(1)}, bf16[3,128,128]{2,1,0:T(8,128)(2,1)S(1)}, u32[]{:S(2)}, u32[]{:S(2)}) %collective-permute-start.5) | collective-permute-done | bytes 98336 | tf_op jit(solution)/shard_map/ppermute | solution.py:21
  69.0 4.2 %collective-permute-start.6 = (bf16[22,3,128]{2,1,0:T(4,128)(2,1)S(1)}, bf16[22,3,128]{2,1,0:T(4,128)(2,1)S(1)}, u32[]{:S(2)}, u32[]{:S(2)}) collective-permute-start(bf16[22,3,128]{2,1,0:T(4,128)(2,1)S(1)} %get-tuple-element.66), channel_id=1, source_target_pairs={{0,1},{2,3},{4,5},{6,7},{8,9},{10,11},{12,13},{14,15},{16,17},{18,... | collective-permute-start | bytes 50696 | tf_op jit(solution)/shard_map/ppermute | solution.py:20
  73.3 1.5 collective-permute-start.7
  74.7 0.0 copy-done.1
  74.8 0.0 copy-done.6
  74.8 3.1 %fusion.8 = bf16[2048,128]{1,0:T(8,128)(2,1)} fusion(bf16[2048,512]{1,0:T(8,128)(2,1)} %copy-done, bf16[512,128]{1,0:T(8,128)(2,1)S(1)} %all_gather.7, bf16[2048,128]{1,0:T(8,128)(2,1)S(1)} %bitcast.185, f32[128]{0:T(128)S(1)} %copy-done.6), kind=kOutput, calls=%fused_computation.62 | convolution fusion | flops 269484032 | bytes 3277312 | tf_op jit(solution)/shard_map/dot_general | solution.py:98
  77.9 0.1 stack.199
  78.0 40.0 %all-reduce = (f32[512]{0:T(512)}, f32[7,7,128]{2,1,0:T(8,128)}, f32[128]{0:T(128)}) all-reduce(f32[512]{0:T(512)S(1)} %get-tuple-element.127, f32[7,7,128]{2,1,0:T(8,128)S(1)} %reshape.62, f32[128]{0:T(128)S(1)} %get-tuple-element.56), channel_id=1, replica_groups=mesh['fsdp'=2,'rows'=8,'cols'=2] {'fsdp','rows','cols'}, use_global_device_ids=true, to_apply=%region_7.0 | all-reduce | flops 6912 | bytes 55296 | tf_op jit(solution)/shard_map/psum | solution.py:141
  118.0 0.0 collective-permute-done.6
  118.0 0.0 collective-permute-done.7
  118.0 0.2 maximum_convert_fusion.1
  118.3 0.0 copy-done.3
  118.3 8.1 %fusion.108 = bf16[1,16,128,128]{3,2,1,0:T(8,128)(2,1)} fusion(f32[128]{0:T(128)S(1)} %get-tuple-element.121, f32[22,134,128]{2,1,0:T(8,128)S(1)} %maximum_convert_fusion.1, f32[128]{0:T(128)S(1)} %get-tuple-element.122, f32[128]{0:T(128)S(1)} %get-tuple-element.75, f32[128]{0:T(128)S(1)} %get-tuple-element.76, f32[128]{0:T(128)S(1)} %get-tuple-element.77, ...), kind=kLoop, calls=%fused_computation.221 | loop fusion | flops 26214400 | bytes 52453888 | tf_op jit(solution)/shard_map/broadcast_in_dim | solution.py:147
  126.4 71.1 %all-reduce.4.cloned.1.call-done = (f32[128,512]{1,0:T(8,128)}, f32[512,128]{1,0:T(8,128)}) async-done(((f32[128,512]{1,0:T(8,128)}, f32[512,128]{1,0:T(8,128)}), (f32[128,512]{1,0:T(8,128)}, f32[512,128]{1,0:T(8,128)})) %all-reduce.4.cloned.1.call-update) | async-done | bytes 524304 | tf_op jit(solution)/shard_map/psum | solution.py:141
  197.5 1.6 constant_dynamic-slice_fusion
  199.1 1.6 constant_dynamic-slice_fusion.1
  (7 shorter events, 0.1 us)
Async XLA Ops:
  7.2 190.3 %all-reduce.4.cloned.1.call-start = ((), (), s32[]{:S(2)}) async-start(), calls=%async_computation | async-start | bytes 1048576 | tf_op jit(solution)/shard_map/psum | solution.py:141
  8.2 13.4 %collective-permute-start = (bf16[3,128,128]{2,1,0:T(8,128)(2,1)S(1)}, bf16[3,128,128]{2,1,0:T(8,128)(2,1)S(1)}, u32[]{:S(2)}, u32[]{:S(2)}) collective-permute-start(bf16[3,128,128]{2,1,0:T(8,128)(2,1)S(1)} %get-tuple-element.72), channel_id=1, source_target_pairs={{0,2},{2,4},{4,6},{6,8},{8,10},{10,12},{12,14},{1,3},{3,5},{5,7},{... | collective-permute-start | bytes 294920 | tf_op jit(solution)/shard_map/ppermute | solution.py:20
  12.8 8.8 %collective-permute-start.1 = (bf16[3,128,128]{2,1,0:T(8,128)(2,1)S(1)}, bf16[3,128,128]{2,1,0:T(8,128)(2,1)S(1)}, u32[]{:S(2)}, u32[]{:S(2)}) collective-permute-start(bf16[3,128,128]{2,1,0:T(8,128)(2,1)S(1)} %get-tuple-element.73), channel_id=1, source_target_pairs={{2,0},{4,2},{6,4},{8,6},{10,8},{12,10},{14,12},{3,1},{5,3},{7,5},{... | collective-permute-start | bytes 294920 | tf_op jit(solution)/shard_map/ppermute | solution.py:21
  22.4 9.3 %collective-permute-start.2 = (bf16[22,3,128]{2,1,0:T(4,128)(2,1)S(1)}, bf16[22,3,128]{2,1,0:T(4,128)(2,1)S(1)}, u32[]{:S(2)}, u32[]{:S(2)}) collective-permute-start(bf16[22,3,128]{2,1,0:T(4,128)(2,1)S(1)} %get-tuple-element.68), channel_id=1, source_target_pairs={{0,1},{2,3},{4,5},{6,7},{8,9},{10,11},{12,13},{14,15},{16,17},{18,... | collective-permute-start | bytes 50696 | tf_op jit(solution)/shard_map/ppermute | solution.py:20
  25.5 6.1 %collective-permute-start.3 = (bf16[22,3,128]{2,1,0:T(4,128)(2,1)S(1)}, bf16[22,3,128]{2,1,0:T(4,128)(2,1)S(1)}, u32[]{:S(2)}, u32[]{:S(2)}) collective-permute-start(bf16[22,3,128]{2,1,0:T(4,128)(2,1)S(1)} %get-tuple-element.69), channel_id=1, source_target_pairs={{1,0},{3,2},{5,4},{7,6},{9,8},{11,10},{13,12},{15,14},{17,16},{19,... | collective-permute-start | bytes 50696 | tf_op jit(solution)/shard_map/ppermute | solution.py:21
  32.9 8.9 %copy-start.4 = (f32[128]{0:T(128)S(1)}, f32[128]{0:T(128)}, u32[]{:S(2)}) copy-start(f32[128]{0:T(128)} %param.13) | copy-start | bytes 1540
  32.9 8.9 %copy-start.5 = (f32[128]{0:T(128)S(1)}, f32[128]{0:T(128)}, u32[]{:S(2)}) copy-start(f32[128]{0:T(128)} %param.14) | copy-start | bytes 1540
  32.9 9.5 %copy-start.7 = (f32[512]{0:T(512)S(1)}, f32[512]{0:T(512)}, u32[]{:S(2)}) copy-start(f32[512]{0:T(512)} %param.16) | copy-start | bytes 6148
  42.5 1.8 copy-start.2
  44.3 20.7 %copy-start = (bf16[2048,512]{1,0:T(8,128)(2,1)}, bf16[2048,512]{1,0:T(8,128)(2,1)S(1)}, u32[]{:S(2)}) copy-start(bf16[2048,512]{1,0:T(8,128)(2,1)S(1)} %get-tuple-element.123) | copy-start | bytes 6291460
  56.4 18.3 %copy-start.1 = (bf16[1,16,128,128]{3,2,1,0:T(8,128)(2,1)S(1)}, bf16[1,16,128,128]{3,2,1,0:T(8,128)(2,1)}, u32[]{:S(2)}) copy-start(bf16[1,16,128,128]{3,2,1,0:T(8,128)(2,1)} %param.10) | copy-start | bytes 1572868
  56.5 18.3 %copy-start.6 = (f32[128]{0:T(128)S(1)}, f32[128]{0:T(128)}, u32[]{:S(2)}) copy-start(f32[128]{0:T(128)} %param.18) | copy-start | bytes 1540
  57.7 8.8 %collective-permute-start.4 = (bf16[3,128,128]{2,1,0:T(8,128)(2,1)S(1)}, bf16[3,128,128]{2,1,0:T(8,128)(2,1)S(1)}, u32[]{:S(2)}, u32[]{:S(2)}) collective-permute-start(bf16[3,128,128]{2,1,0:T(8,128)(2,1)S(1)} %get-tuple-element.70), channel_id=1, source_target_pairs={{0,2},{2,4},{4,6},{6,8},{8,10},{10,12},{12,14},{1,3},{3,5},{5,7},{... | collective-permute-start | bytes 294920 | tf_op jit(solution)/shard_map/ppermute | solution.py:20
  63.0 5.9 %collective-permute-start.5 = (bf16[3,128,128]{2,1,0:T(8,128)(2,1)S(1)}, bf16[3,128,128]{2,1,0:T(8,128)(2,1)S(1)}, u32[]{:S(2)}, u32[]{:S(2)}) collective-permute-start(bf16[3,128,128]{2,1,0:T(8,128)(2,1)S(1)} %get-tuple-element.71), channel_id=1, source_target_pairs={{2,0},{4,2},{6,4},{8,6},{10,8},{12,10},{14,12},{3,1},{5,3},{7,5},{... | collective-permute-start | bytes 294920 | tf_op jit(solution)/shard_map/ppermute | solution.py:21
  66.4 51.8 %copy-start.3 = (bf16[1,16,128,128]{3,2,1,0:T(8,128)(2,1)S(1)}, bf16[1,16,128,128]{3,2,1,0:T(8,128)(2,1)}, u32[]{:S(2)}) copy-start(bf16[1,16,128,128]{3,2,1,0:T(8,128)(2,1)} %param.19) | copy-start | bytes 1572868
  69.0 49.0 %collective-permute-start.6 = (bf16[22,3,128]{2,1,0:T(4,128)(2,1)S(1)}, bf16[22,3,128]{2,1,0:T(4,128)(2,1)S(1)}, u32[]{:S(2)}, u32[]{:S(2)}) collective-permute-start(bf16[22,3,128]{2,1,0:T(4,128)(2,1)S(1)} %get-tuple-element.66), channel_id=1, source_target_pairs={{0,1},{2,3},{4,5},{6,7},{8,9},{10,11},{12,13},{14,15},{16,17},{18,... | collective-permute-start | bytes 50696 | tf_op jit(solution)/shard_map/ppermute | solution.py:20
  73.3 44.8 %collective-permute-start.7 = (bf16[22,3,128]{2,1,0:T(4,128)(2,1)S(1)}, bf16[22,3,128]{2,1,0:T(4,128)(2,1)S(1)}, u32[]{:S(2)}, u32[]{:S(2)}) collective-permute-start(bf16[22,3,128]{2,1,0:T(4,128)(2,1)S(1)} %get-tuple-element.67), channel_id=1, source_target_pairs={{1,0},{3,2},{5,4},{7,6},{9,8},{11,10},{13,12},{15,14},{17,16},{19,... | collective-permute-start | bytes 50696 | tf_op jit(solution)/shard_map/ppermute | solution.py:21
Sparse Core Ops, SparseCore 0:
  66.6 130.8 all-reduce.3
where the time goes:
time: 210 us; the launch traced here: 207 us
  waiting for transfers between devices  73.6 us (35%)
  blocking collectives  48.8 us (23%)
  other arithmetic  28 us (13%)
  starting transfers between devices  24 us (11%)
  between operations  14.4 us (7%)
  matrix products  11.5 us (5%)
  local copies, waits for them, and re-layouts  7.18 us (3%)
    psum x1, waiting for transfers between devices, on_device(): lax.psum((term_in, term_out, bias_term, kernel_term, gain_product), ('fsd...  71.1 us
    psum x1, blocking collectives, on_device(): lax.psum((term_in, term_out, bias_term, kernel_term, gain_product), ('fsd...  40 us
    ppermute x4, starting transfers between devices, padded_2(): before = lax.ppermute(last, axis, up)  17.3 us
    reduce_sum x1, other arithmetic, on_device(): center = jnp.mean(conv, axis=-1, keepdims=True)  8.22 us
    broadcast_in_dim x1, other arithmetic, on_device(): d_image[None]  8.14 us
    reduce_sum x3, other arithmetic, on_device(): jnp.sum(padded_f[row_tap:row_tap + height, col_tap:col_tap + width] * con...  7.12 us
    ppermute x4, starting transfers between devices, padded_2(): after = lax.ppermute(leading, axis, down)  6.61 us
    all_gather x1, blocking collectives, on_device(): lax.all_gather(w_out, 'fsdp', axis=0, tiled=True)  4.84 us
  transfers between devices with their start and end apart: 9, of which 2 were waited for; matrix products, arithmetic and copies ran while one was open for 8% of the time, Pallas kernels for 0%

commit v1 on v0

v1 whole, which is shorter than its diff:
```python
import functools
import math

import jax
import jax.numpy as jnp
from jax import lax
from jax.experimental import pallas as pl
from jax.experimental.pallas import tpu as pltpu
from jax.sharding import PartitionSpec as P

norm_eps = 1e-06
gelu_coef = math.sqrt(2.0 / math.pi)
cubic_coef = 0.044715
EDGE = 8
F32 = jnp.float32
BF16 = jnp.bfloat16
VMEM = pl.BlockSpec(memory_space=pltpu.VMEM)


def pair_perm(count, first):
    perm = []
    for i in range(first, count - 1, 2):
        perm += [(i, i + 1), (i + 1, i)]
    return perm


def call(kernel, out_shape, scratch=(), cost=None, limit=40 << 20):
    return pl.pallas_call(
        kernel,
        out_shape=out_shape,
        scratch_shapes=scratch,
        compiler_params=pltpu.CompilerParams(vmem_limit_bytes=limit),
        cost_estimate=cost,
    )


def odd(axis):
    return lax.rem(lax.axis_index(axis), 2) == 1


def pick(cond, yes, no):
    return jnp.where(cond, yes.astype(F32), no.astype(F32)).astype(yes.dtype)


def pack_first(image_ref, w_in_ref, w_out_ref, w_pack_ref, *col_refs):
    width = image_ref.shape[1]
    depth, hid = w_in_ref.shape
    for i in range(hid // 128):
        w_pack_ref[i * depth : (i + 1) * depth, :] = w_in_ref[:, i * 128 : (i + 1) * 128]
    w_pack_ref[depth * hid // 128 :, :] = w_out_ref[...]
    pack_cols(image_ref, col_refs)


def pack_cols(field_ref, col_refs):
    width = field_ref.shape[1]
    is_odd = odd("cols")
    left = field_ref[:, 0:EDGE, :]
    right = field_ref[:, width - EDGE : width, :]
    col_refs[0][...] = pick(is_odd, left, right)
    if len(col_refs) > 1:
        col_refs[1][...] = pick(is_odd, right, left)


def col_sides(col_refs):
    is_odd = odd("cols")
    got_a = col_refs[0][...]
    got_b = col_refs[1][...] if len(col_refs) > 1 else jnp.zeros_like(got_a)
    return pick(is_odd, got_a, got_b), pick(is_odd, got_b, got_a)


def pack_rows(n_col, field_ref, *refs):
    col_refs, (row_a, row_b) = refs[:n_col], refs[n_col:]
    height, width, _ = field_ref.shape
    left, right = col_sides(col_refs)
    is_odd = odd("rows")
    for ref, want_top in ((row_a, is_odd), (row_b, jnp.logical_not(is_odd))):
        ref[:, 0:EDGE, :] = pick(want_top, left[0:3], left[height - 3 :])
        ref[:, EDGE : EDGE + width, :] = pick(want_top, field_ref[0:3], field_ref[height - 3 :])
        ref[:, EDGE + width :, :] = pick(want_top, right[0:3], right[height - 3 :])


def fill_padded(padded, field_ref, col_refs, row_a, row_b):
    height, width, _ = field_ref.shape
    left, right = col_sides(col_refs)
    is_odd = odd("rows")
    padded[3 : 3 + height, 0:EDGE, :] = left.astype(F32)
    padded[3 : 3 + height, EDGE + width :, :] = right.astype(F32)

    def row(i, _):
        padded[3 + i, EDGE : EDGE + width, :] = field_ref[i].astype(F32)
        return 0

    lax.fori_loop(0, height, row, 0)
    got_a, got_b = row_a[...].astype(F32), row_b[...].astype(F32)
    padded[0:3] = jnp.where(is_odd, got_a, got_b)
    padded[3 + height :] = jnp.where(is_odd, got_b, got_a)


def taps_of_row(padded, kernel_ref, row, width, flip):
    total = None
    for a in range(7):
        for b in range(7):
            tap = (6 - a) * 7 + 6 - b if flip else a * 7 + b
            term = padded[row + a, pl.ds(EDGE - 3 + b, width), :] * kernel_ref[tap : tap + 1, :]
            total = term if total is None else total + term
    return total


def main_kernel(n_col, rows_at_once, *refs):
    image_ref = refs[0]
    col_refs = refs[1 : 1 + n_col]
    (
        row_a, row_b, kernel_ref, dw_bias_ref, gain_ref, bias_ref, w_in_ref, b_in_ref, w_out_ref,
        b_out_ref, w_got_ref, cot_ref,
        mixed_ref, dconv_ref, own_ref, other_ref,
    ) = refs[1 + n_col : 17 + n_col]
    outs = refs[17 + n_col :]
    dcol_refs = outs[:n_col]
    padded, full_in, full_out, sum_in, sum_out, sum_bias, sum_gain = outs[n_col:]
    height, width, chan = image_ref.shape
    hid = w_in_ref.shape[1]
    in_rows, out_rows = w_in_ref.shape[0], w_out_ref.shape[0]
    me = lax.axis_index("fsdp")
    fill_padded(padded, image_ref, col_refs, row_a, row_b)

    def at(which, size):
        return pl.ds(pl.multiple_of(which * size, size), size)

    full_in[at(me, in_rows), :] = w_in_ref[...]
    for i in range(hid // 128):
        full_in[at(1 - me, in_rows), i * 128 : (i + 1) * 128] = w_got_ref[
            i * in_rows : (i + 1) * in_rows, :
        ]
    full_out[at(me, out_rows), :] = w_out_ref[...]
    full_out[at(1 - me, out_rows), :] = w_got_ref[in_rows * hid // 128 :, :]
    sum_in[...] = jnp.zeros_like(sum_in)
    sum_out[...] = jnp.zeros_like(sum_out)
    sum_bias[...] = jnp.zeros_like(sum_bias)
    sum_gain[...] = jnp.zeros_like(sum_gain)
    gain = gain_ref[...]
    pixels = rows_at_once * width
    half = hid // 2
    nn = (((1,), (0,)), ((), ()))
    nt = (((1,), (1,)), ((), ()))
    tn = (((0,), (0,)), ((), ()))

    def dot(x, y, dims):
        return lax.dot_general(x, y, dims, preferred_element_type=F32)

    def block(i, _):
        first = i * rows_at_once
        conv = jnp.concatenate(
            [
                taps_of_row(padded, kernel_ref, first + j, width, False)
                for j in range(rows_at_once)
            ],
            axis=0,
        ) + dw_bias_ref[...]
        center = jnp.mean(conv, axis=-1, keepdims=True)
        spread = conv - center
        rstd = lax.rsqrt(jnp.mean(spread * spread, axis=-1, keepdims=True) + norm_eps)
        xhat = spread * rstd
        normed = (xhat * gain + bias_ref[...]).astype(BF16)
        upstream = cot_ref[pl.ds(first, rows_at_once)].reshape(pixels, chan)
        field = image_ref[pl.ds(first, rows_at_once)].reshape(pixels, chan)
        mixed = field.astype(F32) + b_out_ref[...]
        back = jnp.zeros((pixels, chan), F32)
        ones = jnp.ones((8, pixels), BF16)
        for h in range(2):
            cols = slice(h * half, (h + 1) * half)
            wi, wo = full_in[:, cols], full_out[cols, :]
            pre = dot(normed, wi, nn) + b_in_ref[:, cols]
            square = pre * pre
            tanh = jnp.tanh(pre * (gelu_coef + (gelu_coef * cubic_coef) * square))
            up_tanh = 1.0 + tanh
            half_pre = 0.5 * pre
            hidden = (half_pre * up_tanh).astype(BF16)
            slope = up_tanh * (
                0.5
                + half_pre
                * (1.0 - tanh)
                * (gelu_coef + (3.0 * gelu_coef * cubic_coef) * square)
            )
            mixed = mixed + dot(hidden, wo, nn)
            d_pre = (dot(upstream, wo, nt) * slope).astype(BF16)
            back = back + dot(d_pre, wi, nt)
            sum_in[:, cols] += dot(normed, d_pre, tn)
            sum_out[:, cols] += dot(upstream, hidden, tn)
            sum_bias[:, cols] += dot(ones, d_pre, nn)
        mixed_ref[pl.ds(first, rows_at_once)] = mixed.astype(BF16).reshape(rows_at_once, width, chan)
        sum_gain[...] += jnp.sum((back * xhat).reshape(pixels // 8, 8, chan), axis=0)
        q = back * gain
        d_conv = rstd * (
            q
            - jnp.mean(q, axis=-1, keepdims=True)
            - xhat * jnp.mean(q * xhat, axis=-1, keepdims=True)
        )
        dconv_ref[pl.ds(first, rows_at_once)] = d_conv.astype(BF16).reshape(
            rows_at_once, width, chan
        )
        return 0

    lax.fori_loop(0, height // rows_at_once, block, 0)
    pack_cols(dconv_ref, dcol_refs)

    base = in_rows * hid // 128 + out_rows
    for ref, which in ((own_ref, me), (other_ref, 1 - me)):
        for i in range(hid // 128):
            ref[i * in_rows : (i + 1) * in_rows, :] = sum_in[
                at(which, in_rows), i * 128 : (i + 1) * 128
            ].astype(BF16)
        ref[in_rows * hid // 128 : base, :] = (
            sum_out[:, at(which, out_rows)].T.astype(BF16)
        )
    small = [sum_bias[0:1, i * 128 : (i + 1) * 128] for i in range(hid // 128)]
    small.append(jnp.sum(sum_gain[...], axis=0, keepdims=True))
    for a in range(7):

        def row(r, sums):
            grad = dconv_ref[r].astype(F32)
            return tuple(
                sums[b]
                + jnp.sum(
                    (padded[r + a, pl.ds(EDGE - 3 + b, width), :] * grad).reshape(
                        width // 8, 8, chan
                    ),
                    axis=0,
                )
                for b in range(7)
            )

        sums = lax.fori_loop(0, height, row, (jnp.zeros((8, chan), F32),) * 7)
        small += [jnp.sum(s, axis=0, keepdims=True) for s in sums]
    small = jnp.concatenate(small, axis=0)
    pad = own_ref.shape[0] - base - small.shape[0]
    small = jnp.concatenate([small, jnp.zeros((pad, chan), F32)], axis=0).astype(BF16)
    own_ref[base:, :] = small
    other_ref[base:, :] = small


def image_kernel(n_col, *refs):
    dconv_ref = refs[0]
    col_refs = refs[1 : 1 + n_col]
    row_a, row_b, kernel_ref, cot_ref, out_ref, padded = refs[1 + n_col :]
    height, width, _ = dconv_ref.shape
    fill_padded(padded, dconv_ref, col_refs, row_a, row_b)

    def row(r, _):
        total = taps_of_row(padded, kernel_ref, r, width, True)
        out_ref[r] = (cot_ref[r].astype(F32) + total).astype(BF16)
        return 0

    lax.fori_loop(0, height, row, 0)


def finish_kernel(acc_ref, got_ref, g_in_ref, g_out_ref, g_b_ref, g_k_ref, g_gain_ref):
    in_rows, hid = g_in_ref.shape
    total = acc_ref[...].astype(F32) + got_ref[...].astype(F32)
    for i in range(hid // 128):
        g_in_ref[:, i * 128 : (i + 1) * 128] = total[i * in_rows : (i + 1) * in_rows]
    base = in_rows * hid // 128
    g_out_ref[...] = total[base : base + g_out_ref.shape[0]]
    base += g_out_ref.shape[0]
    for i in range(hid // 128):
        g_b_ref[:, i * 128 : (i + 1) * 128] = total[base + i : base + i + 1]
    base += hid // 128
    g_gain_ref[...] = total[base : base + 1]
    for a in range(7):
        g_k_ref[a] = total[base + 1 + 7 * a : base + 8 + 7 * a]


def on_device(sizes, image, dw_kernel, dw_bias, gain, bias, w_in, b_in, w_out, b_out, cotangent):
    n_fsdp, n_rows, n_cols = sizes
    field, upstream = image[0], cotangent[0]
    height, width, chan = field.shape
    in_rows, hid = w_in.shape
    out_rows = w_out.shape[0]
    shape = jax.ShapeDtypeStruct
    n_col = 2 if n_cols > 2 else 1
    col_shape = shape((height, EDGE, chan), BF16)
    row_shape = shape((3, width + 2 * EDGE, chan), BF16)
    field_shape = shape((height, width, chan), BF16)
    taps = dw_kernel.reshape(49, chan)

    def swap_cols(edges):
        return [lax.ppermute(e, "cols", pair_perm(n_cols, i)) for i, e in enumerate(edges)]

    def swap_rows(edges):
        return [lax.ppermute(e, "rows", pair_perm(n_rows, i)) for i, e in enumerate(edges)]

    w_rows = in_rows * hid // 128 + out_rows
    w_pack, *cols = call(pack_first, (shape((w_rows, 128), BF16),) + (col_shape,) * n_col)(
        field, w_in, w_out
    )
    cols = swap_cols(cols)
    w_got = lax.ppermute(w_pack, "fsdp", pair_perm(n_fsdp, 0))
    rows = call(functools.partial(pack_rows, n_col), (row_shape,) * 2)(field, *cols)
    rows = swap_rows(rows)
    n_small = hid // 128 + 1 + 49
    pack_shape = shape((w_rows + -(-n_small // 16) * 16, 128), BF16)
    padded = pltpu.VMEM((height + 6, width + 2 * EDGE, chan), F32)
    row1 = lambda v: v.reshape(1, -1)
    mixed, d_conv, own, other, *d_cols = call(
        functools.partial(main_kernel, n_col, 2),
        (field_shape, field_shape, pack_shape, pack_shape) + (col_shape,) * n_col,
        scratch=[
            padded,
            pltpu.VMEM((in_rows * n_fsdp, hid), BF16),
            pltpu.VMEM((out_rows * n_fsdp, chan), BF16),
            pltpu.VMEM((chan, hid), F32),
            pltpu.VMEM((chan, hid), F32),
            pltpu.VMEM((8, hid), F32),
            pltpu.VMEM((8, chan), F32),
        ],
    )(
        field, *cols, *rows, taps, row1(dw_bias), row1(gain), row1(bias), w_in, row1(b_in), w_out,
        row1(b_out), w_got, upstream,
    )
    d_cols = swap_cols(d_cols)
    d_rows = call(functools.partial(pack_rows, n_col), (row_shape,) * 2)(d_conv, *d_cols)
    d_rows = swap_rows(d_rows)
    d_image = call(functools.partial(image_kernel, n_col), field_shape, scratch=[padded])(
        d_conv, *d_cols, *d_rows, taps, upstream
    )

    got = lax.ppermute(other, "fsdp", pair_perm(n_fsdp, 0))
    acc = own
    bits = [("cols", 1 << i) for i in range(n_cols.bit_length() - 1)]
    bits += [("rows", 1 << i) for i in range(n_rows.bit_length() - 1)]
    for axis, bit in bits:
        acc = (acc.astype(F32) + got.astype(F32)).astype(BF16)
        count = n_rows if axis == "rows" else n_cols
        got = lax.ppermute(acc, axis, [(i, i ^ bit) for i in range(count)])
    g_in, g_out, g_b, g_k, g_gain = call(
        finish_kernel,
        (
            shape((in_rows, hid), F32),
            shape((out_rows, chan), F32),
            shape((1, hid), F32),
            shape((7, 7, chan), F32),
            shape((1, chan), F32),
        ),
    )(acc, got)
    return (
        mixed[None], d_image[None], g_in, g_out, g_b.reshape(-1), g_k, g_gain.reshape(-1),
    )


def solution(mesh):
    sizes = tuple(mesh.shape[name] for name in ("fsdp", "rows", "cols"))
    if sizes[0] != 2 or any(n & (n - 1) for n in sizes):
        raise ValueError(sizes)
    blocks = P("fsdp", "rows", "cols", None)
    return jax.shard_map(
        functools.partial(on_device, sizes),
        mesh=mesh,
        in_specs=(
            blocks, P(), P(), P(), P(), P("fsdp", None), P(), P("fsdp", None), P(), blocks,
        ),
        out_specs=(blocks, blocks, P("fsdp", None), P("fsdp", None), P(), P(), P()),
        check_vma=False,
    )
```

time: 210 us -> 73.1 us (0.35); the launches traced: 207 us -> 72.7 us
  waiting for transfers between devices: 73.6 us -> 18.4 us
  blocking collectives: 48.8 us -> 0 us
  other arithmetic: 28 us -> 0.17 us
  Pallas kernels: 0 us -> 25.1 us
  between operations: 14.4 us -> 0.81 us
  matrix products: 11.5 us -> 0 us
  local copies, waits for them, and re-layouts: 7.18 us -> 3.39 us
    psum x1 -> x0, waiting for transfers between devices: 71.1 us -> none  [on_device(): lax.psum((term_in, term_out, bias_term, kernel_term, gain_product), ('fsd...]
    psum x1 -> x0, blocking collectives: 40 us -> none  [on_device(): lax.psum((term_in, term_out, bias_term, kernel_term, gain_product), ('fsd...]
    pallas_call x0 -> x6, Pallas kernels: none -> 25.1 us  [the longest x1 19 us: on_device(): call(functools.partial(main_kernel, n_col, 2), (field_shape, field_shape,...]
    reduce_sum x6 -> x0, other arithmetic: 17 us -> none  [the longest x1 8.22 us: on_device(): center = jnp.mean(conv, axis=-1, keepdims=True)]
    ppermute x8 -> x12, waiting for transfers between devices: 2.52 us -> 18.4 us  [the longest x4 7.75 us: on_device(): got = lax.ppermute(acc, axis, [(i, i ^ bit) for i in range(count)])]
    dot_general x6 -> x0, matrix products: 11.5 us -> none  [the longest x1 3.13 us: on_device(): lax.dot_general(flat_up, full_out, contract_cols, preferred_element_type=...]
    all_gather x2 -> x0, blocking collectives: 8.83 us -> none  [the longest x1 4.84 us: on_device(): lax.all_gather(w_out, 'fsdp', axis=0, tiled=True)]
    broadcast_in_dim x1 -> x0, other arithmetic: 8.14 us -> none  [on_device(): d_image[None]]
  transfers between devices with their start and end apart: 9 -> 12, of which waited for: 2 -> 8; matrix products, arithmetic and copies ran while one was open for 8% -> 0% of each run, Pallas kernels for 0% -> 7%
where the time goes in v1:
time: 73.1 us; the launch traced here: 72.7 us
  Pallas kernels  25.1 us (34%)
  starting transfers between devices  24.9 us (34%)
  waiting for transfers between devices  18.4 us (25%)
  local copies, waits for them, and re-layouts  3.39 us (5%)
  between operations  0.81 us (1%)
    pallas_call x1, Pallas kernels, on_device(): call(functools.partial(main_kernel, n_col, 2), (field_shape, field_shape,...  19 us
    ppermute x4, starting transfers between devices, swap_rows(): lax.ppermute(e, 'rows', pair_perm(n_rows, i))  9.87 us
    ppermute x4, starting transfers between devices, on_device(): got = lax.ppermute(acc, axis, [(i, i ^ bit) for i in range(count)])  8.73 us
    ppermute x4, waiting for transfers between devices, on_device(): got = lax.ppermute(acc, axis, [(i, i ^ bit) for i in range(count)])  7.75 us
    ppermute x4, waiting for transfers between devices, swap_rows(): lax.ppermute(e, 'rows', pair_perm(n_rows, i))  6.5 us
    pallas_call x1, Pallas kernels, on_device(): call(functools.partial(image_kernel, n_col), field_shape, scratch=[padded])  5.18 us
    unnamed x26, local copies, waits for them, and re-layouts  3.39 us
    ppermute x2, starting transfers between devices, swap_cols(): lax.ppermute(e, 'cols', pair_perm(n_cols, i))  3.3 us
  transfers between devices with their start and end apart: 12, of which 8 were waited for; matrix products, arithmetic and copies ran while one was open for 0% of the time, Pallas kernels for 7%

profile of v1, /device:TPU:1, one launch (start us, length us, event | category | flops | bytes accessed | tf_op | source)
XLA Modules:
  0.0 72.7 jit_solution(12731466110861246852)
XLA Ops:
  0.6 0.0 copy-start
  0.6 1.0 %copy-done = bf16[1,16,128,128]{3,2,1,0:T(8,128)(2,1)S(1)} copy-done((bf16[1,16,128,128]{3,2,1,0:T(8,128)(2,1)S(1)}, bf16[1,16,128,128]{3,2,1,0:T(8,128)(2,1)}, u32[]{:S(2)}) %copy-start) | copy-done | bytes 524312
  1.7 0.0 copy-start.3
  1.7 0.8 %copy-done.3 = bf16[64,512]{1,0:T(8,128)(2,1)S(1)} copy-done((bf16[64,512]{1,0:T(8,128)(2,1)S(1)}, bf16[64,512]{1,0:T(8,128)(2,1)}, u32[]{:S(2)}) %copy-start.3) | copy-done | bytes 65560
  2.5 0.0 copy-start.5
  2.5 0.8 %copy-done.5 = bf16[256,128]{1,0:T(8,128)(2,1)S(1)} copy-done((bf16[256,128]{1,0:T(8,128)(2,1)S(1)}, bf16[256,128]{1,0:T(8,128)(2,1)}, u32[]{:S(2)}) %copy-start.5) | copy-done | bytes 65560
  3.4 0.0 copy-start.1
  3.4 0.0 copy-start.2
  3.4 2.1 %collective-permute-start = (bf16[16,8,128]{2,1,0:T(8,128)(2,1)S(1)}, bf16[16,8,128]{2,1,0:T(8,128)(2,1)S(1)}, u32[]{:S(2)}, u32[]{:S(2)}) collective-permute-start(bf16[16,8,128]{2,1,0:T(8,128)(2,1)S(1)} %get-tuple-element.23), channel_id=1, source_target_pairs={{0,1},{1,0},{2,3},{3,2},{4,5},{5,4},{6,7},{7,6},{8,9},{9,8},{10,11... | collective-permute-start | bytes 98312 | tf_op jit(solution)/shard_map/ppermute | solution.py:286
  5.5 0.0 copy-start.12
  5.5 1.2 %collective-permute-start.3 = (bf16[512,128]{1,0:T(8,128)(2,1)S(1)}, bf16[512,128]{1,0:T(8,128)(2,1)S(1)}, u32[]{:S(2)}, u32[]{:S(2)}) collective-permute-start(bf16[512,128]{1,0:T(8,128)(2,1)S(1)} %get-tuple-element.26), channel_id=1, source_target_pairs={{0,16},{16,0},{1,17},{17,1},{2,18},{18,2},{3,19},{19,3},{4,20},{20... | collective-permute-start | bytes 393224 | tf_op jit(solution)/shard_map/ppermute | solution.py:296
  6.7 0.1 collective-permute-done.refs_0_.refs_1_
  6.8 0.0 copy-start.6
  6.8 0.1 shard_map.154
  6.9 0.0 copy-start.4
  6.9 1.6 %collective-permute-start.1 = (bf16[3,144,128]{2,1,0:T(8,128)(2,1)S(1)}, bf16[3,144,128]{2,1,0:T(8,128)(2,1)S(1)}, u32[]{:S(2)}, u32[]{:S(2)}) collective-permute-start(bf16[3,144,128]{2,1,0:T(8,128)(2,1)S(1)} %get-tuple-element.24), channel_id=1, source_target_pairs={{0,2},{2,0},{4,6},{6,4},{8,10},{10,8},{12,14},{14,12},{1,3},{3,1},... | collective-permute-start | bytes 331784 | tf_op jit(solution)/shard_map/ppermute | solution.py:289
  8.5 3.6 %collective-permute-start.2 = (bf16[3,144,128]{2,1,0:T(8,128)(2,1)S(1)}, bf16[3,144,128]{2,1,0:T(8,128)(2,1)S(1)}, u32[]{:S(2)}, u32[]{:S(2)}) collective-permute-start(bf16[3,144,128]{2,1,0:T(8,128)(2,1)S(1)} %get-tuple-element.25), channel_id=1, source_target_pairs={{2,4},{4,2},{6,8},{8,6},{10,12},{12,10},{3,5},{5,3},{7,9},{9,7},{1... | collective-permute-start | bytes 331784 | tf_op jit(solution)/shard_map/ppermute | solution.py:289
  12.1 0.0 copy-done.12
  12.1 0.0 copy-start.11
  12.2 0.0 collective-permute-done.3.refs_12_
  12.2 0.0 collective-permute-done.1.refs_2_
  12.2 2.4 %collective-permute-done.2.refs_3_ = bf16[3,144,128]{2,1,0:T(8,128)(2,1)S(1)} collective-permute-done((bf16[3,144,128]{2,1,0:T(8,128)(2,1)S(1)}, bf16[3,144,128]{2,1,0:T(8,128)(2,1)S(1)}, u32[]{:S(2)}, u32[]{:S(2)}) %collective-permute-start.2) | collective-permute-done | bytes 110624 | tf_op jit(solution)/shard_map/ppermute | solution.py:289
  14.5 0.0 copy-start.7
  14.5 0.0 copy-start.8
  14.5 0.0 copy-start.9
  14.5 0.0 copy-start.10
  14.6 0.0 copy-done.1
  14.6 0.0 copy-done.2
  14.6 0.0 copy-done.6
  14.6 0.0 copy-done.4
  14.6 0.0 copy-done.11
  14.6 0.6 copy-done.7
  15.2 0.0 copy-done.8
  15.2 0.0 copy-done.9
  15.2 0.0 copy-done.10
  15.2 19.0 %shard_map.155 = (bf16[16,128,128]{2,1,0:T(8,128)(2,1)}, bf16[16,128,128]{2,1,0:T(8,128)(2,1)S(1)}, bf16[576,128]{1,0:T(8,128)(2,1)S(1)}, bf16[576,128]{1,0:T(8,128)(2,1)S(1)}, bf16[16,8,128]{2,1,0:T(8,128)(2,1)S(1)}) custom-call(bf16[16,128,128]{2,1,0:T(8,128)(2,1)S(1)} %bitcast.13, bf16[16,8,128]{2,1,0:T(8,128)(2,1)S(1)} %collective-permute-done.refs_0_.refs_1_, ...), custom_call_target="tpu_custom_call" | custom-call | tf_op jit(solution)/shard_map/pallas_call | solution.py:303
  34.2 1.8 %collective-permute-start.7 = (bf16[576,128]{1,0:T(8,128)(2,1)S(1)}, bf16[576,128]{1,0:T(8,128)(2,1)S(1)}, u32[]{:S(2)}, u32[]{:S(2)}) collective-permute-start(bf16[576,128]{1,0:T(8,128)(2,1)S(1)} %get-tuple-element.33), channel_id=1, source_target_pairs={{0,16},{16,0},{1,17},{17,1},{2,18},{18,2},{3,19},{19,3},{4,20},{20... | collective-permute-start | bytes 442376 | tf_op jit(solution)/shard_map/ppermute | solution.py:326
  36.0 2.5 %collective-permute-done.7 = bf16[576,128]{1,0:T(8,128)(2,1)S(1)} collective-permute-done((bf16[576,128]{1,0:T(8,128)(2,1)S(1)}, bf16[576,128]{1,0:T(8,128)(2,1)S(1)}, u32[]{:S(2)}, u32[]{:S(2)}) %collective-permute-start.7) | collective-permute-done | bytes 147488 | tf_op jit(solution)/shard_map/ppermute | solution.py:326
  38.6 1.8 %collective-permute-start.8 = (bf16[576,128]{1,0:T(8,128)(2,1)S(1)}, bf16[576,128]{1,0:T(8,128)(2,1)S(1)}, u32[]{:S(2)}, u32[]{:S(2)}) collective-permute-start(bf16[576,128]{1,0:T(8,128)(2,1)S(1)} %add_convert_fusion.3), channel_id=1, source_target_pairs={{0,1},{1,0},{2,3},{3,2},{4,5},{5,4},{6,7},{7,6},{8,9},{9,8},{10,11... | collective-permute-start | bytes 442376 | tf_op jit(solution)/shard_map/ppermute | solution.py:333
  40.4 2.5 %collective-permute-done.8 = bf16[576,128]{1,0:T(8,128)(2,1)S(1)} collective-permute-done((bf16[576,128]{1,0:T(8,128)(2,1)S(1)}, bf16[576,128]{1,0:T(8,128)(2,1)S(1)}, u32[]{:S(2)}, u32[]{:S(2)}) %collective-permute-start.8) | collective-permute-done | bytes 147488 | tf_op jit(solution)/shard_map/ppermute | solution.py:333
  42.9 0.1 collective-permute-start.9
  43.0 1.4 %collective-permute-done.9 = bf16[576,128]{1,0:T(8,128)(2,1)S(1)} collective-permute-done((bf16[576,128]{1,0:T(8,128)(2,1)S(1)}, bf16[576,128]{1,0:T(8,128)(2,1)S(1)}, u32[]{:S(2)}, u32[]{:S(2)}) %collective-permute-start.9) | collective-permute-done | bytes 147488 | tf_op jit(solution)/shard_map/ppermute | solution.py:333
  44.4 4.6 %collective-permute-start.10 = (bf16[576,128]{1,0:T(8,128)(2,1)S(1)}, bf16[576,128]{1,0:T(8,128)(2,1)S(1)}, u32[]{:S(2)}, u32[]{:S(2)}) collective-permute-start(bf16[576,128]{1,0:T(8,128)(2,1)S(1)} %add_convert_fusion.1), channel_id=1, source_target_pairs={{0,4},{2,6},{4,0},{6,2},{8,12},{10,14},{12,8},{14,10},{1,5},{3,7},... | collective-permute-start | bytes 442376 | tf_op jit(solution)/shard_map/ppermute | solution.py:333
  49.0 3.9 %collective-permute-done.10 = bf16[576,128]{1,0:T(8,128)(2,1)S(1)} collective-permute-done((bf16[576,128]{1,0:T(8,128)(2,1)S(1)}, bf16[576,128]{1,0:T(8,128)(2,1)S(1)}, u32[]{:S(2)}, u32[]{:S(2)}) %collective-permute-start.10) | collective-permute-done | bytes 147488 | tf_op jit(solution)/shard_map/ppermute | solution.py:333
  52.9 2.3 %collective-permute-start.11 = (bf16[576,128]{1,0:T(8,128)(2,1)S(1)}, bf16[576,128]{1,0:T(8,128)(2,1)S(1)}, u32[]{:S(2)}, u32[]{:S(2)}) collective-permute-start(bf16[576,128]{1,0:T(8,128)(2,1)S(1)} %add_convert_fusion.acc_ref), channel_id=1, source_target_pairs={{0,8},{2,10},{4,12},{6,14},{8,0},{10,2},{12,4},{14,6},{1,9},{3,11}... | collective-permute-start | bytes 442376 | tf_op jit(solution)/shard_map/ppermute | solution.py:333
  55.2 1.2 %collective-permute-start.4 = (bf16[16,8,128]{2,1,0:T(8,128)(2,1)S(1)}, bf16[16,8,128]{2,1,0:T(8,128)(2,1)S(1)}, u32[]{:S(2)}, u32[]{:S(2)}) collective-permute-start(bf16[16,8,128]{2,1,0:T(8,128)(2,1)S(1)} %get-tuple-element.29), channel_id=1, source_target_pairs={{0,1},{1,0},{2,3},{3,2},{4,5},{5,4},{6,7},{7,6},{8,9},{9,8},{10,11... | collective-permute-start | bytes 98312 | tf_op jit(solution)/shard_map/ppermute | solution.py:286
  56.4 1.6 %collective-permute-done.4.refs_0_.refs_1_ = bf16[16,8,128]{2,1,0:T(8,128)(2,1)S(1)} collective-permute-done((bf16[16,8,128]{2,1,0:T(8,128)(2,1)S(1)}, bf16[16,8,128]{2,1,0:T(8,128)(2,1)S(1)}, u32[]{:S(2)}, u32[]{:S(2)}) %collective-permute-start.4) | collective-permute-done | bytes 32800 | tf_op jit(solution)/shard_map/ppermute | solution.py:286
  58.0 0.1 shard_map.156
  58.0 2.7 %collective-permute-start.5 = (bf16[3,144,128]{2,1,0:T(8,128)(2,1)S(1)}, bf16[3,144,128]{2,1,0:T(8,128)(2,1)S(1)}, u32[]{:S(2)}, u32[]{:S(2)}) collective-permute-start(bf16[3,144,128]{2,1,0:T(8,128)(2,1)S(1)} %get-tuple-element.30), channel_id=1, source_target_pairs={{0,2},{2,0},{4,6},{6,4},{8,10},{10,8},{12,14},{14,12},{1,3},{3,1},... | collective-permute-start | bytes 331784 | tf_op jit(solution)/shard_map/ppermute | solution.py:289
  60.8 1.9 %collective-permute-start.6 = (bf16[3,144,128]{2,1,0:T(8,128)(2,1)S(1)}, bf16[3,144,128]{2,1,0:T(8,128)(2,1)S(1)}, u32[]{:S(2)}, u32[]{:S(2)}) collective-permute-start(bf16[3,144,128]{2,1,0:T(8,128)(2,1)S(1)} %get-tuple-element.31), channel_id=1, source_target_pairs={{2,4},{4,2},{6,8},{8,6},{10,12},{12,10},{3,5},{5,3},{7,9},{9,7},{1... | collective-permute-start | bytes 331784 | tf_op jit(solution)/shard_map/ppermute | solution.py:289
  62.7 0.0 collective-permute-done.5.refs_2_
  62.7 4.1 %collective-permute-done.6.refs_3_ = bf16[3,144,128]{2,1,0:T(8,128)(2,1)S(1)} collective-permute-done((bf16[3,144,128]{2,1,0:T(8,128)(2,1)S(1)}, bf16[3,144,128]{2,1,0:T(8,128)(2,1)S(1)}, u32[]{:S(2)}, u32[]{:S(2)}) %collective-permute-start.6) | collective-permute-done | bytes 110624 | tf_op jit(solution)/shard_map/ppermute | solution.py:289
  66.8 5.2 %shard_map.157 = bf16[16,128,128]{2,1,0:T(8,128)(2,1)} custom-call(bf16[16,128,128]{2,1,0:T(8,128)(2,1)S(1)} %get-tuple-element.28.field_ref.refs_0_, bf16[16,8,128]{2,1,0:T(8,128)(2,1)S(1)} %collective-permute-done.4.refs_0_.refs_1_, bf16[3,144,128]{2,1,0:T(8,128)(2,1)S(1)} %collective-permute-done.5.refs_2_, ...), custom_call_target="tpu_custom_call" | custom-call | tf_op jit(solution)/shard_map/pallas_call | solution.py:322
  72.0 0.0 collective-permute-done.11.got_ref
  72.0 0.7 %shard_map.158 = (f32[64,512]{1,0:T(8,128)}, f32[256,128]{1,0:T(8,128)}, f32[1,512]{1,0:T(1,128)}, f32[7,7,128]{2,1,0:T(8,128)}, f32[1,128]{1,0:T(1,128)}) custom-call(bf16[576,128]{1,0:T(8,128)(2,1)S(1)} %add_convert_fusion.acc_ref, bf16[576,128]{1,0:T(8,128)(2,1)S(1)} %collective-permute-done.11.got_ref), custom_call_target="tpu_custom_call" | custom-call | tf_op jit(solution)/shard_map/pallas_call | solution.py:334
  (6 shorter events, 0.2 us)
Async XLA Ops:
  0.6 1.0 %copy-start = (bf16[1,16,128,128]{3,2,1,0:T(8,128)(2,1)S(1)}, bf16[1,16,128,128]{3,2,1,0:T(8,128)(2,1)}, u32[]{:S(2)}) copy-start(bf16[1,16,128,128]{3,2,1,0:T(8,128)(2,1)} %param.10) | copy-start | bytes 1572868
  1.7 0.8 %copy-start.3 = (bf16[64,512]{1,0:T(8,128)(2,1)S(1)}, bf16[64,512]{1,0:T(8,128)(2,1)}, u32[]{:S(2)}) copy-start(bf16[64,512]{1,0:T(8,128)(2,1)} %refs_8_.1) | copy-start | bytes 196612
  2.5 0.8 %copy-start.5 = (bf16[256,128]{1,0:T(8,128)(2,1)S(1)}, bf16[256,128]{1,0:T(8,128)(2,1)}, u32[]{:S(2)}) copy-start(bf16[256,128]{1,0:T(8,128)(2,1)} %refs_10_.1) | copy-start | bytes 196612
  3.4 11.2 %copy-start.1 = (bf16[1,16,128,128]{3,2,1,0:T(8,128)(2,1)S(1)}, bf16[1,16,128,128]{3,2,1,0:T(8,128)(2,1)}, u32[]{:S(2)}) copy-start(bf16[1,16,128,128]{3,2,1,0:T(8,128)(2,1)} %param.10) | copy-start | bytes 1572868
  3.4 11.2 %copy-start.2 = (bf16[1,16,128,128]{3,2,1,0:T(8,128)(2,1)S(1)}, bf16[1,16,128,128]{3,2,1,0:T(8,128)(2,1)}, u32[]{:S(2)}) copy-start(bf16[1,16,128,128]{3,2,1,0:T(8,128)(2,1)} %param.19) | copy-start | bytes 1572868
  3.4 3.4 %collective-permute-start = (bf16[16,8,128]{2,1,0:T(8,128)(2,1)S(1)}, bf16[16,8,128]{2,1,0:T(8,128)(2,1)S(1)}, u32[]{:S(2)}, u32[]{:S(2)}) collective-permute-start(bf16[16,8,128]{2,1,0:T(8,128)(2,1)S(1)} %get-tuple-element.23), channel_id=1, source_target_pairs={{0,1},{1,0},{2,3},{3,2},{4,5},{5,4},{6,7},{7,6},{8,9},{9,8},{10,11... | collective-permute-start | bytes 98312 | tf_op jit(solution)/shard_map/ppermute | solution.py:286
  5.5 6.6 %copy-start.12 = (f32[7,7,128]{2,1,0:T(8,128)S(1)}, f32[7,7,128]{2,1,0:T(8,128)}, u32[]{:S(2)}) copy-start(f32[7,7,128]{2,1,0:T(8,128)} %param.11) | copy-start | bytes 75268
  5.5 6.7 %collective-permute-start.3 = (bf16[512,128]{1,0:T(8,128)(2,1)S(1)}, bf16[512,128]{1,0:T(8,128)(2,1)S(1)}, u32[]{:S(2)}, u32[]{:S(2)}) collective-permute-start(bf16[512,128]{1,0:T(8,128)(2,1)S(1)} %get-tuple-element.26), channel_id=1, source_target_pairs={{0,16},{16,0},{1,17},{17,1},{2,18},{18,2},{3,19},{19,3},{4,20},{20... | collective-permute-start | bytes 393224 | tf_op jit(solution)/shard_map/ppermute | solution.py:296
  6.8 7.8 %copy-start.6 = (bf16[256,128]{1,0:T(8,128)(2,1)S(1)}, bf16[256,128]{1,0:T(8,128)(2,1)}, u32[]{:S(2)}) copy-start(bf16[256,128]{1,0:T(8,128)(2,1)} %refs_10_.1) | copy-start | bytes 196612
  6.9 7.7 %copy-start.4 = (bf16[64,512]{1,0:T(8,128)(2,1)S(1)}, bf16[64,512]{1,0:T(8,128)(2,1)}, u32[]{:S(2)}) copy-start(bf16[64,512]{1,0:T(8,128)(2,1)} %refs_8_.1) | copy-start | bytes 196612
  6.9 5.3 %collective-permute-start.1 = (bf16[3,144,128]{2,1,0:T(8,128)(2,1)S(1)}, bf16[3,144,128]{2,1,0:T(8,128)(2,1)S(1)}, u32[]{:S(2)}, u32[]{:S(2)}) collective-permute-start(bf16[3,144,128]{2,1,0:T(8,128)(2,1)S(1)} %get-tuple-element.24), channel_id=1, source_target_pairs={{0,2},{2,0},{4,6},{6,4},{8,10},{10,8},{12,14},{14,12},{1,3},{3,1},... | collective-permute-start | bytes 331784 | tf_op jit(solution)/shard_map/ppermute | solution.py:289
  8.5 6.1 %collective-permute-start.2 = (bf16[3,144,128]{2,1,0:T(8,128)(2,1)S(1)}, bf16[3,144,128]{2,1,0:T(8,128)(2,1)S(1)}, u32[]{:S(2)}, u32[]{:S(2)}) collective-permute-start(bf16[3,144,128]{2,1,0:T(8,128)(2,1)S(1)} %get-tuple-element.25), channel_id=1, source_target_pairs={{2,4},{4,2},{6,8},{8,6},{10,12},{12,10},{3,5},{5,3},{7,9},{9,7},{1... | collective-permute-start | bytes 331784 | tf_op jit(solution)/shard_map/ppermute | solution.py:289
  12.1 2.5 %copy-start.11 = (f32[128]{0:T(128)S(1)}, f32[128]{0:T(128)}, u32[]{:S(2)}) copy-start(f32[128]{0:T(128)} %param.18) | copy-start | bytes 1540
  14.5 0.7 copy-start.7
  14.5 0.7 copy-start.8
  14.5 0.7 copy-start.9
  14.5 0.7 copy-start.10
  34.2 4.3 %collective-permute-start.7 = (bf16[576,128]{1,0:T(8,128)(2,1)S(1)}, bf16[576,128]{1,0:T(8,128)(2,1)S(1)}, u32[]{:S(2)}, u32[]{:S(2)}) collective-permute-start(bf16[576,128]{1,0:T(8,128)(2,1)S(1)} %get-tuple-element.33), channel_id=1, source_target_pairs={{0,16},{16,0},{1,17},{17,1},{2,18},{18,2},{3,19},{19,3},{4,20},{20... | collective-permute-start | bytes 442376 | tf_op jit(solution)/shard_map/ppermute | solution.py:326
  38.6 4.3 %collective-permute-start.8 = (bf16[576,128]{1,0:T(8,128)(2,1)S(1)}, bf16[576,128]{1,0:T(8,128)(2,1)S(1)}, u32[]{:S(2)}, u32[]{:S(2)}) collective-permute-start(bf16[576,128]{1,0:T(8,128)(2,1)S(1)} %add_convert_fusion.3), channel_id=1, source_target_pairs={{0,1},{1,0},{2,3},{3,2},{4,5},{5,4},{6,7},{7,6},{8,9},{9,8},{10,11... | collective-permute-start | bytes 442376 | tf_op jit(solution)/shard_map/ppermute | solution.py:333
  42.9 1.4 %collective-permute-start.9 = (bf16[576,128]{1,0:T(8,128)(2,1)S(1)}, bf16[576,128]{1,0:T(8,128)(2,1)S(1)}, u32[]{:S(2)}, u32[]{:S(2)}) collective-permute-start(bf16[576,128]{1,0:T(8,128)(2,1)S(1)} %add_convert_fusion.2), channel_id=1, source_target_pairs={{0,2},{2,0},{4,6},{6,4},{8,10},{10,8},{12,14},{14,12},{1,3},{3,1},... | collective-permute-start | bytes 442376 | tf_op jit(solution)/shard_map/ppermute | solution.py:333
  44.4 8.5 %collective-permute-start.10 = (bf16[576,128]{1,0:T(8,128)(2,1)S(1)}, bf16[576,128]{1,0:T(8,128)(2,1)S(1)}, u32[]{:S(2)}, u32[]{:S(2)}) collective-permute-start(bf16[576,128]{1,0:T(8,128)(2,1)S(1)} %add_convert_fusion.1), channel_id=1, source_target_pairs={{0,4},{2,6},{4,0},{6,2},{8,12},{10,14},{12,8},{14,10},{1,5},{3,7},... | collective-permute-start | bytes 442376 | tf_op jit(solution)/shard_map/ppermute | solution.py:333
  52.9 19.1 %collective-permute-start.11 = (bf16[576,128]{1,0:T(8,128)(2,1)S(1)}, bf16[576,128]{1,0:T(8,128)(2,1)S(1)}, u32[]{:S(2)}, u32[]{:S(2)}) collective-permute-start(bf16[576,128]{1,0:T(8,128)(2,1)S(1)} %add_convert_fusion.acc_ref), channel_id=1, source_target_pairs={{0,8},{2,10},{4,12},{6,14},{8,0},{10,2},{12,4},{14,6},{1,9},{3,11}... | collective-permute-start | bytes 442376 | tf_op jit(solution)/shard_map/ppermute | solution.py:333
  55.2 2.8 %collective-permute-start.4 = (bf16[16,8,128]{2,1,0:T(8,128)(2,1)S(1)}, bf16[16,8,128]{2,1,0:T(8,128)(2,1)S(1)}, u32[]{:S(2)}, u32[]{:S(2)}) collective-permute-start(bf16[16,8,128]{2,1,0:T(8,128)(2,1)S(1)} %get-tuple-element.29), channel_id=1, source_target_pairs={{0,1},{1,0},{2,3},{3,2},{4,5},{5,4},{6,7},{7,6},{8,9},{9,8},{10,11... | collective-permute-start | bytes 98312 | tf_op jit(solution)/shard_map/ppermute | solution.py:286
  58.0 4.6 %collective-permute-start.5 = (bf16[3,144,128]{2,1,0:T(8,128)(2,1)S(1)}, bf16[3,144,128]{2,1,0:T(8,128)(2,1)S(1)}, u32[]{:S(2)}, u32[]{:S(2)}) collective-permute-start(bf16[3,144,128]{2,1,0:T(8,128)(2,1)S(1)} %get-tuple-element.30), channel_id=1, source_target_pairs={{0,2},{2,0},{4,6},{6,4},{8,10},{10,8},{12,14},{14,12},{1,3},{3,1},... | collective-permute-start | bytes 331784 | tf_op jit(solution)/shard_map/ppermute | solution.py:289
  60.8 6.1 %collective-permute-start.6 = (bf16[3,144,128]{2,1,0:T(8,128)(2,1)S(1)}, bf16[3,144,128]{2,1,0:T(8,128)(2,1)S(1)}, u32[]{:S(2)}, u32[]{:S(2)}) collective-permute-start(bf16[3,144,128]{2,1,0:T(8,128)(2,1)S(1)} %get-tuple-element.31), channel_id=1, source_target_pairs={{2,4},{4,2},{6,8},{8,6},{10,12},{12,10},{3,5},{5,3},{7,9},{9,7},{1... | collective-permute-start | bytes 331784 | tf_op jit(solution)/shard_map/ppermute | solution.py:289
